TPU v7x, 256 devices: a whole 4x4x8 slice. The times are simulated.
256 devices in a mesh: sens: 4 (over z_lo, core), par: 64 (over z_hi, x, y).
Axes of the slice: x: 4, y: 4, z: 8 (z_hi: 4, z_lo: 2; z = z_hi * 2 + z_lo), core: 2. Of those that a mesh axis runs over, the one named last changes fastest.
Arguments:
- model: bfloat16 [4, 1024, 256], P('sens', 'par'), may hold values from -6 to 6
- kernel: bfloat16 [512, 1024, 256], P('sens', 'par'), may hold values from -0.01171875 to 0.01171875
- observed: float32 [4, 512, 256], P(None, 'sens'), may hold values from -6 to 6
- weights: float32 [512], P('sens'), may hold values from 0.25 to 4
Outputs:
- gradient: float32 [4, 1024, 256], P('sens', 'par')
- misfit: float32 [], replicated
All inputs are finite; a program needn't handle non-finite values.
Results may differ from a plain program's by a relative error of at most 0.0027.
Values may be sent and summed in bfloat16 or wider, within the bound.
A program may use at most 192 MiB of HBM per device.

v0:
```python
import jax
import jax.numpy as jnp
from jax import lax
from jax.sharding import PartitionSpec as P


def causal_rows(series):
    length_steps = series.shape[-1]
    padded = jnp.concatenate([series, jnp.zeros_like(series)], axis=-1)
    reps = (1,) * (series.ndim - 1) + (length_steps,)
    flat = jnp.tile(padded, reps)
    stride = 2 * length_steps - 1
    flat = flat[..., : length_steps * stride].reshape(series.shape[:-1] + (length_steps, stride))
    return flat[..., :length_steps]


def leading_rows(series):
    length_steps = series.shape[-1]
    padded = jnp.concatenate([series, jnp.zeros_like(series)], axis=-1)
    reps = (1,) * (series.ndim - 1) + (length_steps + 1,)
    flat = jnp.tile(padded, reps)
    stride = 2 * length_steps + 1
    flat = flat[..., : length_steps * stride].reshape(series.shape[:-1] + (length_steps, stride))
    return flat[..., :length_steps]


def local(model, kernel, observed, weights):
    full_model = lax.all_gather(model, "sens", axis=0, tiled=True)
    toeplitz_operator = causal_rows(full_model)
    summed_terms = jnp.einsum(
        "oua,luaz->loz", kernel, toeplitz_operator, preferred_element_type=jnp.float32
    )
    vectors = full_model.shape[0]
    sensors = weights.shape[0]
    steps = full_model.shape[2]
    entries = vectors * sensors * lax.axis_size("sens") * steps
    predicted = lax.psum(summed_terms, "par")
    mismatch = predicted - observed
    weighted_residual = weights[None, :, None] * mismatch
    residual = weighted_residual.astype(jnp.bfloat16)
    squared = lax.psum(jnp.sum(weighted_residual * mismatch), "sens")
    misfit = 0.5 * squared / entries

    def single_adjoint(series):
        shifted = leading_rows(series)
        return jnp.einsum("spk,skt->pt", kernel, shifted, preferred_element_type=jnp.float32)

    adjoint_pieces = lax.map(single_adjoint, residual)
    gradient = lax.psum_scatter(adjoint_pieces, "sens", scatter_dimension=0, tiled=True)
    return (gradient, misfit)


def solution(mesh):
    return jax.shard_map(
        local,
        mesh=mesh,
        in_specs=(P("sens", "par", None), P("sens", "par", None), P(None, "sens", None), P("sens")),
        out_specs=(P("sens", "par", None), P()),
        check_vma=False,
    )
```

profile of v0, /device:TPU:1, one launch (start us, length us, event | category | flops | bytes accessed | tf_op | source)
XLA Modules:
  0.0 1190.9 jit_solution(9768342964295590249)
XLA Ops:
  7.2 0.0 all-reduce.4.cloned.1.call-start
  7.2 8.4 all_gather.3
  15.7 5.9 tile.8
  21.6 17.0 %tile.9 = bf16[4,16,131072]{2,1,0:T(8,128)(2,1)} reshape(bf16[4,16,256,512]{3,2,1,0:T(8,128)(2,1)} %tile.8) | data formatting | bytes 33554432 | tf_op jit(solution)/shard_map/tile | solution.py:11
  38.6 13.7 %slice.16 = bf16[4,16,130816]{2,1,0:T(8,128)(2,1)} slice(bf16[4,16,131072]{2,1,0:T(8,128)(2,1)} %tile.9), slice={[0:4], [0:16], [0:130816]} | slice | bytes 33488896 | tf_op jit(solution)/shard_map/slice | solution.py:13
  52.3 0.0 copy-start
  52.3 36.2 %reshape.19 = bf16[4,16,256,511]{3,2,1,0:T(8,128)(2,1)} reshape(bf16[4,16,130816]{2,1,0:T(8,128)(2,1)} %slice.16) | data formatting | bytes 33488896 | tf_op jit(solution)/shard_map/reshape | solution.py:13
  88.5 0.0 copy-done
  88.5 0.0 copy-start.1
  88.5 0.0 copy-start.2
  88.5 6.6 fusion.10
  95.1 0.0 all-reduce.4.cloned.1.call-update
  95.1 0.0 reduce-scatter.2.cloned.1.call-start
  95.2 1.6 copy.19
  96.8 0.0 copy-done.1
  96.8 0.2 copy.18
  97.0 688.3 %all-reduce.4.cloned.1.call-done = f32[4,128,256]{1,2,0:T(8,128)} async-done(((f32[4,128,256]{1,2,0:T(8,128)}), f32[4,128,256]{1,2,0:T(8,128)}) %all-reduce.4.cloned.1.call-update) | async-done | bytes 524304 | tf_op jit(solution)/shard_map/psum | solution.py:37
  785.3 0.0 copy-done.2
  785.3 1.9 fusion.15
  787.2 332.0 %while.10 = (s32[]{:T(128)}, f32[4,16,256]{2,1,0:T(8,128)}, bf16[4,128,256]{1,2,0:T(8,128)(2,1)S(1)}, bf16[128,16,256]{0,1,2:T(8,128)(2,1)S(1)}, s32[]{:T(128)}, /*index=5*/bf16[]{:T(256)}) while((s32[]{:T(128)}, f32[4,16,256]{2,1,0:T(8,128)}, bf16[4,128,256]{1,2,0:T(8,128)(2,1)S(1)}, bf16[128,16,256]{0,1,2:T(8,128)(2,1)S(1)}, s32[]{:T(128)}, ...), condition=%wide.region_2.0_spmd, body=%wide.region_1.0_spmd.sunk | while | flops 268435456 | bytes 186466896 | solution.py:48
  787.2 13.5 %tile.21 = bf16[128,257,512]{0,2,1:T(8,128)(2,1)} broadcast(bf16[128,512]{0,1:T(8,128)(2,1)S(1)} %concatenate.8), dimensions={0,2} | broadcast | bytes 33816576 | tf_op jit(solution)/shard_map/while/body/eval_jaxpr/tile | solution.py:21
  800.8 22.9 %slice.31 = bf16[128,131328]{0,1:T(8,128)(2,1)} slice(bf16[128,131584]{0,1:T(8,128)(2,1)} %bitcast.32), slice={[0:128], [0:131328]} | slice | bytes 67239936 | tf_op jit(solution)/shard_map/while/body/eval_jaxpr/slice | solution.py:23
  823.6 37.7 %reshape.24 = bf16[128,256,513]{0,2,1:T(8,128)(2,1)} reshape(bf16[128,131328]{0,1:T(8,128)(2,1)} %slice.31) | data formatting | bytes 67239936 | tf_op jit(solution)/shard_map/while/body/eval_jaxpr/reshape | solution.py:23
  861.3 8.9 fusion.22
  870.2 13.5 %tile.21 = bf16[128,257,512]{0,2,1:T(8,128)(2,1)} broadcast(bf16[128,512]{0,1:T(8,128)(2,1)S(1)} %concatenate.8), dimensions={0,2} | broadcast | bytes 33816576 | tf_op jit(solution)/shard_map/while/body/eval_jaxpr/tile | solution.py:21
  883.7 22.9 %slice.31 = bf16[128,131328]{0,1:T(8,128)(2,1)} slice(bf16[128,131584]{0,1:T(8,128)(2,1)} %bitcast.32), slice={[0:128], [0:131328]} | slice | bytes 67239936 | tf_op jit(solution)/shard_map/while/body/eval_jaxpr/slice | solution.py:23
  906.6 37.7 %reshape.24 = bf16[128,256,513]{0,2,1:T(8,128)(2,1)} reshape(bf16[128,131328]{0,1:T(8,128)(2,1)} %slice.31) | data formatting | bytes 67239936 | tf_op jit(solution)/shard_map/while/body/eval_jaxpr/reshape | solution.py:23
  944.3 8.9 fusion.22
  953.2 13.5 %tile.21 = bf16[128,257,512]{0,2,1:T(8,128)(2,1)} broadcast(bf16[128,512]{0,1:T(8,128)(2,1)S(1)} %concatenate.8), dimensions={0,2} | broadcast | bytes 33816576 | tf_op jit(solution)/shard_map/while/body/eval_jaxpr/tile | solution.py:21
  966.7 22.9 %slice.31 = bf16[128,131328]{0,1:T(8,128)(2,1)} slice(bf16[128,131584]{0,1:T(8,128)(2,1)} %bitcast.32), slice={[0:128], [0:131328]} | slice | bytes 67239936 | tf_op jit(solution)/shard_map/while/body/eval_jaxpr/slice | solution.py:23
  989.6 37.7 %reshape.24 = bf16[128,256,513]{0,2,1:T(8,128)(2,1)} reshape(bf16[128,131328]{0,1:T(8,128)(2,1)} %slice.31) | data formatting | bytes 67239936 | tf_op jit(solution)/shard_map/while/body/eval_jaxpr/reshape | solution.py:23
  1027.2 8.9 fusion.22
  1036.2 13.5 %tile.21 = bf16[128,257,512]{0,2,1:T(8,128)(2,1)} broadcast(bf16[128,512]{0,1:T(8,128)(2,1)S(1)} %concatenate.8), dimensions={0,2} | broadcast | bytes 33816576 | tf_op jit(solution)/shard_map/while/body/eval_jaxpr/tile | solution.py:21
  1049.7 22.9 %slice.31 = bf16[128,131328]{0,1:T(8,128)(2,1)} slice(bf16[128,131584]{0,1:T(8,128)(2,1)} %bitcast.32), slice={[0:128], [0:131328]} | slice | bytes 67239936 | tf_op jit(solution)/shard_map/while/body/eval_jaxpr/slice | solution.py:23
  1072.6 37.7 %reshape.24 = bf16[128,256,513]{0,2,1:T(8,128)(2,1)} reshape(bf16[128,131328]{0,1:T(8,128)(2,1)} %slice.31) | data formatting | bytes 67239936 | tf_op jit(solution)/shard_map/while/body/eval_jaxpr/reshape | solution.py:23
  1110.2 8.9 fusion.22
  1119.1 0.0 reduce-scatter.2.cloned.1.call-update
  1119.2 51.3 %psum.15 = f32[]{:T(128)} all-reduce(f32[]{:T(128)} %get-tuple-element.45), channel_id=1, replica_groups=mesh['sens'=4,'par'=64] {'sens'}, use_global_device_ids=true, to_apply=%region_5.6 | all-reduce | flops 1 | bytes 8 | tf_op jit(solution)/shard_map/psum | solution.py:41
  1171.1 11.8 reduce-scatter.2.cloned.1.call-done
  (10 shorter events, 0.1 us)
Async XLA Ops:
  7.2 778.2 %all-reduce.4.cloned.1.call-start = ((), (), s32[]{:S(2)}) async-start(), calls=%async_computation.1 | async-start | bytes 1048576 | tf_op jit(solution)/shard_map/psum | solution.py:37
  52.3 36.2 %copy-start = (bf16[128,16,256]{2,1,0:T(8,128)(2,1)S(1)}, bf16[128,16,256]{2,1,0:T(8,128)(2,1)}, u32[]{:S(2)}) copy-start(bf16[128,16,256]{2,1,0:T(8,128)(2,1)} %param.7) | copy-start | bytes 3145732
  88.5 8.4 copy-start.1
  88.5 696.9 %copy-start.2 = (f32[128]{0:T(128)S(1)}, f32[128]{0:T(128)}, u32[]{:S(2)}) copy-start(f32[128]{0:T(128)} %param.9) | copy-start | bytes 1540
  95.1 1087.8 %reduce-scatter.2.cloned.1.call-start = ((), (), s32[]{:S(2)}) async-start(), calls=%async_computation.2 | async-start | bytes 81920 | tf_op jit(solution)/shard_map/reduce_scatter | solution.py:49
Sparse Core Ops, SparseCore 0:
  95.2 690.0 all-reduce.3
  1119.3 63.6 reduce-scatter.1
where the time goes:
time: 1200 us; the launch traced here: 1190 us
  waiting for transfers between devices  700 us (58%)
  local copies, waits for them, and re-layouts  371 us (31%)
  blocking collectives  59.7 us (5%)
  matrix products  42.3 us (4%)
  between operations  15.9 us (1%)
    psum x1, waiting for transfers between devices, local(): predicted = lax.psum(summed_terms, 'par')  688 us
    reshape x4, local copies, waits for them, and re-layouts, leading_rows(): flat[..., :length_steps * stride]  151 us
    slice x4, local copies, waits for them, and re-layouts, leading_rows(): flat[..., :length_steps * stride]  91.4 us
    another operation x4, local copies, waits for them, and re-layouts, leading_rows(): flat = jnp.tile(padded, reps)  54.2 us
    psum x1, blocking collectives, local(): squared = lax.psum(jnp.sum(weighted_residual * mismatch), 'sens')  51.3 us
    reshape x1, local copies, waits for them, and re-layouts, causal_rows(): flat[..., :length_steps * stride]  36.2 us
    dot_general x4, matrix products, single_adjoint(): jnp.einsum('spk,skt->pt', kernel, shifted, preferred_element_type=jnp.flo...  35.6 us
  transfers between devices with their start and end apart: 2, of which 2 were waited for; matrix products, arithmetic and copies ran while one was open for 0% of the time, Pallas kernels for 0%

commit v1 on v0

v1 whole, which is shorter than its diff:
```python
import functools

import jax
import jax.numpy as jnp
from jax import lax
from jax.experimental import pallas as pl
from jax.experimental.pallas import tpu as pltpu
from jax.sharding import PartitionSpec as P

MESH = pl.DeviceIdType.MESH
F32 = jnp.float32
BF16 = jnp.bfloat16
NX = 4
NY = 4
B = 16
ORDER = (2, 1, 3)


def nt(a, b):
    return lax.dot_general(a, b, (((1,), (1,)), ((), ())), preferred_element_type=F32)


def nn(a, b):
    return jnp.dot(a, b, preferred_element_type=F32)


def kernel(
    nz,
    scale,
    model_ref,
    kern_ref,
    obs_ref,
    w_ref,
    grad_ref,
    mis_ref,
    kv,
    kp,
    kt,
    w2,
    eye,
    swap,
    mg,
    xp,
    o0,
    o1,
    ot,
    s0,
    s1,
    r0,
    r1,
    a0,
    a1,
    q0,
    q1,
    zb,
    rf,
    rp,
    mq,
    mr,
    gs,
    gr,
    lsem,
    ssem,
    rsem,
):
    g = lax.axis_index("sens")
    par = lax.axis_index("par")
    z = par // (NX * NY)
    x = (par // NY) % NX
    y = par % NY

    def at_sens(d):
        return {"sens": (g + d) % 4, "par": par}

    def at_x(d):
        return {"sens": g, "par": (z * NX + (x + d) % NX) * NY + y}

    def at_y(d):
        return {"sens": g, "par": (z * NX + x) * NY + (y + d) % NY}

    def at_z(d):
        return {"sens": g, "par": (((z + d) % nz) * NX + x) * NY + y}

    counter = [0]
    pending = []

    def phase():
        base = counter[0]
        counter[0] += 3
        return base

    def send(base, d, src, dst, to):
        c = pltpu.make_async_remote_copy(
            src_ref=src,
            dst_ref=dst,
            send_sem=ssem.at[base + d - 1],
            recv_sem=rsem.at[base + d - 1],
            device_id=to,
            device_id_type=MESH,
        )
        c.start()
        pending.append(c)
        return c

    loads = []
    for n in range(4):
        c = pltpu.make_async_copy(kern_ref.at[pl.ds(512 * n, 512)], kv.at[pl.ds(512 * n, 512)], lsem.at[n])
        c.start()
        loads.append(c)
    own = pltpu.make_async_copy(model_ref.at[0], mg.at[g], lsem.at[4])
    own.start()
    lo0 = pltpu.make_async_copy(obs_ref.at[x, :, pl.ds(0, 128)], o0, lsem.at[5])
    lo0.start()
    lo1 = pltpu.make_async_copy(obs_ref.at[y, :, pl.ds(128, 128)], o1, lsem.at[6])
    lo1.start()

    barrier = pltpu.get_barrier_semaphore()
    zs = tuple(range(1, nz))
    for d in zs:
        pl.semaphore_signal(barrier, inc=1, device_id=at_z(d), device_id_type=MESH)
    for d in ORDER:
        pl.semaphore_signal(barrier, inc=1, device_id=at_x(d), device_id_type=MESH)
        pl.semaphore_signal(barrier, inc=1, device_id=at_y(d), device_id_type=MESH)
        pl.semaphore_signal(barrier, inc=1, device_id=at_sens(d), device_id_type=MESH)

    rows = lax.broadcasted_iota(jnp.int32, (256, 256), 0)
    cols = lax.broadcasted_iota(jnp.int32, (256, 256), 1)
    eye[...] = jnp.where(rows == cols, 1.0, 0.0).astype(BF16)
    swap[...] = jnp.where((rows % 16) * 16 + rows // 16 == cols, 1.0, 0.0).astype(BF16)
    for v in range(4):
        xp[v, 0:240, :] = jnp.zeros((240, 256), BF16)

    for n in range(4):
        loads[n].wait()
        for m in (2 * n, 2 * n + 1):
            out = nn(swap[...], kv[pl.ds(256 * m, 256), :]).astype(BF16)
            kp[:, pl.ds(16 * m, 16), :] = out.reshape(16, 16, 256)

    pl.semaphore_wait(barrier, 9 + len(zs))
    ph = phase()
    gather = [send(ph, d, model_ref.at[0], mg.at[g], at_sens(d)) for d in ORDER]

    for q in range(8):
        out = nt(eye[...], kp[2 * q : 2 * q + 2].reshape(256, 256)).astype(BF16)
        kt[2 * q] = out[:, :128]
        kt[2 * q + 1] = out[:, 128:]
    for c in range(8):
        lo = kt[:, 32 * c : 32 * c + 16, :].reshape(256, 128)
        hi = kt[:, 32 * c + 16 : 32 * c + 32, :].reshape(256, 128)
        out = nn(swap[...], jnp.concatenate([lo, hi], axis=1)).astype(BF16)
        w2[2 * c] = out[:, :128]
        w2[2 * c + 1] = out[:, 128:]

    lo0.wait()
    ot[0] = o0[...].T
    lo1.wait()
    ot[1] = o1[...].T

    own.wait()
    for c in gather:
        c.wait_recv()

    lane = lax.broadcasted_iota(jnp.int32, (16, 256), 1)
    for v in range(4):
        m = mg[v].astype(F32)
        pieces = [m.astype(BF16)]
        for i in range(1, B):
            pieces.append(jnp.where(lane >= i, pltpu.roll(m, i, axis=1), 0.0).astype(BF16))
        stack = jnp.concatenate(pieces, axis=0)
        xp[v, 240:496, :] = nt(eye[...], stack).astype(BF16)

    def predict(v, h):
        blocks = 8 * (h + 1)
        lhs = jnp.concatenate(
            [xp[v, 240 + 128 * h - 16 * a : 368 + 128 * h - 16 * a, :] for a in range(blocks)], axis=1
        )
        return nn(lhs, w2[0:blocks].reshape(blocks * 256, 128))

    ph0 = phase()
    ph1 = phase()
    in0, in1 = {}, {}
    for d in ORDER:
        s1[d] = predict((y + d) % NY, 1)
        in1[d] = send(ph1, d, s1.at[d], r1.at[d - 1], at_y(d))
        s0[d] = predict((x + d) % NX, 0)
        in0[d] = send(ph0, d, s0.at[d], r0.at[d - 1], at_x(d))
    s1[0] = predict(y, 1)
    s0[0] = predict(x, 0)

    ph2 = phase()
    ph3 = phase()
    for d in ORDER:
        in0[d].wait_recv()
    a0[...] = (s0[0] + r0[0]) + (r0[1] + r0[2])
    in2 = {}
    for d in ORDER:
        rows32 = pl.ds(pl.multiple_of(32 * ((y + d) % NY), 32), 32)
        in2[d] = send(ph2, d, a0.at[rows32], q0.at[d - 1], at_y(d))
    for d in ORDER:
        in1[d].wait_recv()
    a1[...] = (s1[0] + r1[0]) + (r1[1] + r1[2])
    in3 = {}
    for d in ORDER:
        rows32 = pl.ds(pl.multiple_of(32 * ((x + d) % NX), 32), 32)
        in3[d] = send(ph3, d, a1.at[rows32], q1.at[d - 1], at_x(d))

    my = pl.ds(pl.multiple_of(32 * y, 32), 32)
    mx = pl.ds(pl.multiple_of(32 * x, 32), 32)
    ph4 = phase()
    ph5 = phase()
    for d in ORDER:
        in2[d].wait_recv()
    zb[0, z] = (a0[my, :] + q0[0]) + (q0[1] + q0[2])
    in4 = [send(ph4, d, zb.at[0, z], zb.at[0, z], at_z(d)) for d in zs]
    for d in ORDER:
        in3[d].wait_recv()
    zb[1, z] = (a1[mx, :] + q1[0]) + (q1[1] + q1[2])
    in5 = [send(ph5, d, zb.at[1, z], zb.at[1, z], at_z(d)) for d in zs]

    weights = w_ref[...]

    def settle(h, rows32):
        total = zb[h, 0]
        for n in range(1, nz):
            total = total + zb[h, n]
        mismatch = total - ot[h, rows32, :]
        weighted = weights * mismatch
        sq = (weighted * mismatch).reshape(4, 8, 128)
        return weighted.astype(BF16), (sq[0] + sq[1]) + (sq[2] + sq[3])

    ph6 = phase()
    ph7 = phase()
    phq = phase()
    for c in in4:
        c.wait_recv()
    res, sq0 = settle(0, my)
    rf[x, my, :] = res
    in6 = [send(ph6, d, rf.at[x, my], rf.at[x, my], at_y(d)) for d in ORDER]
    for c in in5:
        c.wait_recv()
    res, sq1 = settle(1, mx)
    mx1 = pl.ds(pl.multiple_of(128 + 32 * x, 32), 32)
    rf[y, mx1, :] = res
    in7 = [send(ph7, d, rf.at[y, mx1], rf.at[y, mx1], at_x(d)) for d in ORDER]
    mq[0] = sq0 + sq1
    inq = [send(phq, d, mq.at[0], mr.at[y], at_y(d)) for d in ORDER]
    mr[y] = sq0 + sq1

    ph8 = phase()
    ph9 = phase()
    phr = phase()
    for c in in6:
        c.wait_recv()
    in8 = [send(ph8, d, rf.at[x, 0:128], rf.at[x, 0:128], at_x(d)) for d in ORDER]
    for c in in7:
        c.wait_recv()
    in9 = [send(ph9, d, rf.at[y, 128:256], rf.at[y, 128:256], at_y(d)) for d in ORDER]
    for c in inq:
        c.wait_recv()
    sq = (mr[0] + mr[1]) + (mr[2] + mr[3])
    mq[1] = sq
    inr = [send(phr, d, mq.at[1], mr.at[4 + x], at_x(d)) for d in ORDER]
    mr[4 + x] = sq
    for c in in8 + in9 + inr:
        c.wait_recv()
    sq = (mr[4] + mr[5]) + (mr[6] + mr[7])

    rp[256:272, :] = jnp.zeros((16, 128), F32)

    def adjoint(v):
        rp[0:256, :] = rf[v].astype(F32)
        lhs = jnp.concatenate([rp[i : i + 256, :].astype(BF16) for i in range(B)], axis=1)
        rhs = jnp.concatenate([w2[:, 16 * i : 16 * i + 16, :].reshape(256, 128) for i in range(B)], axis=1)
        out = nt(lhs, rhs)
        total = out[:, :128] + jnp.concatenate([out[128:, 128:], jnp.zeros((128, 128), F32)], axis=0)
        for lanes in (64, 32, 16):
            moved = pltpu.roll(total, 128 - lanes, axis=1)
            total = total + jnp.concatenate([moved[lanes:], jnp.zeros((lanes, 128), F32)], axis=0)
        low = lax.broadcasted_iota(jnp.int32, (32, 128), 1) < 16
        packed = jnp.where(low, total[0:32], 0.0)
        for c in range(1, 8):
            packed = packed + pltpu.roll(jnp.where(low, total[32 * c : 32 * c + 32], 0.0), 16 * c, axis=1)
        return packed

    phg = phase()
    ing = {}
    for d in ORDER:
        gs[d, 0:32, :] = adjoint((g + d) % 4)
        gs[d, 32:40, :] = sq
        ing[d] = send(phg, d, gs.at[d], gr.at[d - 1], at_sens(d))
    mine = adjoint(g)
    for d in ORDER:
        ing[d].wait_recv()
    grad_ref[...] = (mine + gr[0, 0:32]) + (gr[1, 0:32] + gr[2, 0:32])
    total = jnp.zeros((8, 128), F32)
    parts = [sq] + [gr[d - 1, 32:40] for d in (1, 2, 3)]
    for owner in range(4):
        for d in range(4):
            total = total + jnp.where((g + 4 - d) % 4 == owner, parts[d], 0.0)
    mis_ref[...] = jnp.broadcast_to(jnp.sum(total, keepdims=True) * scale, (8, 128))
    for c in pending:
        c.wait_send()


def local(nz, scale, model, kern, observed, weights):
    sems = 60
    grad, mis = pl.pallas_call(
        functools.partial(kernel, nz, scale),
        out_shape=(jax.ShapeDtypeStruct((32, 128), F32), jax.ShapeDtypeStruct((8, 128), F32)),
        in_specs=[pl.BlockSpec(memory_space=pl.ANY)] * 3 + [pl.BlockSpec(memory_space=pltpu.VMEM)],
        out_specs=(pl.BlockSpec(memory_space=pltpu.VMEM),) * 2,
        scratch_shapes=[
            pltpu.VMEM((2048, 256), BF16),
            pltpu.VMEM((16, 128, 256), BF16),
            pltpu.VMEM((16, 256, 128), BF16),
            pltpu.VMEM((16, 256, 128), BF16),
            pltpu.VMEM((256, 256), BF16),
            pltpu.VMEM((256, 256), BF16),
            pltpu.VMEM((4, 16, 256), BF16),
            pltpu.VMEM((4, 496, 256), BF16),
            pltpu.VMEM((128, 128), F32),
            pltpu.VMEM((128, 128), F32),
            pltpu.VMEM((2, 128, 128), F32),
            pltpu.VMEM((4, 128, 128), F32),
            pltpu.VMEM((4, 128, 128), F32),
            pltpu.VMEM((3, 128, 128), F32),
            pltpu.VMEM((3, 128, 128), F32),
            pltpu.VMEM((128, 128), F32),
            pltpu.VMEM((128, 128), F32),
            pltpu.VMEM((3, 32, 128), F32),
            pltpu.VMEM((3, 32, 128), F32),
            pltpu.VMEM((2, nz, 32, 128), F32),
            pltpu.VMEM((4, 256, 128), BF16),
            pltpu.VMEM((272, 128), F32),
            pltpu.VMEM((2, 8, 128), F32),
            pltpu.VMEM((8, 8, 128), F32),
            pltpu.VMEM((4, 40, 128), F32),
            pltpu.VMEM((3, 40, 128), F32),
            pltpu.SemaphoreType.DMA((7,)),
            pltpu.SemaphoreType.DMA((sems,)),
            pltpu.SemaphoreType.DMA((sems,)),
        ],
        compiler_params=pltpu.CompilerParams(collective_id=0, has_side_effects=True),
        name="misfit_adjoint",
    )(model, kern.reshape(2048, 256), observed, weights.reshape(1, 128))
    gradient = grad.reshape(32, 8, 16).transpose(2, 1, 0).reshape(1, 16, 256)
    return gradient, mis[0, 0]


def solution(mesh):
    nz = mesh.shape["par"] // (NX * NY)
    entries = 4 * 128 * mesh.shape["sens"] * 256
    return jax.shard_map(
        functools.partial(local, nz, 0.5 / entries),
        mesh=mesh,
        in_specs=(P("sens", "par", None), P("sens", "par", None), P(None, "sens", None), P("sens")),
        out_specs=(P("sens", "par", None), P()),
        check_vma=False,
    )
```

time: 1200 us -> 47.2 us (0.04)
  waiting for transfers between devices: 700 us -> 0 us
  local copies, waits for them, and re-layouts: 371 us -> 2.71 us
  blocking collectives: 59.7 us -> 0 us
  Pallas kernels: 0 us -> 43.6 us
  matrix products: 42.3 us -> 0 us
  between operations: 15.9 us -> 0.65 us
    psum x1 -> x0, waiting for transfers between devices: 688 us -> none  [local(): predicted = lax.psum(summed_terms, 'par')]
    reshape x5 -> x1, local copies, waits for them, and re-layouts: 187 us -> 0.69 us  [local(): gradient = grad.reshape(32, 8, 16).transpose(2, 1, 0).reshape(1, 16, 256)]
    slice x5 -> x1, local copies, waits for them, and re-layouts: 105 us -> 1.18 us  [local(): return (gradient, mis[0, 0])]
    another operation x6 -> x0, local copies, waits for them, and re-layouts: 77.1 us -> none  [the longest x4 54.2 us: leading_rows(): flat = jnp.tile(padded, reps)]
    psum x1 -> x0, blocking collectives: 51.3 us -> none  [local(): squared = lax.psum(jnp.sum(weighted_residual * mismatch), 'sens')]
    pallas_call x0 -> x1, Pallas kernels: none -> 43.6 us  [local(): pl.pallas_call(functools.partial(kernel, nz, scale), out_shape=(jax.Shape...]
    dot_general x5 -> x0, matrix products: 42.3 us -> none  [the longest x4 35.6 us: single_adjoint(): jnp.einsum('spk,skt->pt', kernel, shifted, preferred_element_type=jnp.flo...]
  transfers between devices with their start and end apart: 2 -> 0, of which waited for: 2 -> 0; matrix products, arithmetic and copies ran while one was open for 0% -> 0% of each run, Pallas kernels for 0% -> 0%
where the time goes in v1:
time: 47.2 us; the launch traced here: 47 us
  Pallas kernels  43.6 us (92%)
  local copies, waits for them, and re-layouts  2.71 us (6%)
  between operations  0.65 us (1%)
    pallas_call x1, Pallas kernels, local(): pl.pallas_call(functools.partial(kernel, nz, scale), out_shape=(jax.Shape...  43.6 us
    slice x1, local copies, waits for them, and re-layouts, local(): return (gradient, mis[0, 0])  1.18 us

profile of v1, /device:TPU:1, one launch (start us, length us, event | category | flops | bytes accessed | tf_op | source)
XLA Modules:
  0.0 47.0 jit_solution(16252650710008514946)
XLA Ops:
  0.6 43.6 %misfit_adjoint.1 = (f32[32,128]{1,0:T(8,128)}, f32[8,128]{1,0:T(8,128)}) custom-call(bf16[1,16,256]{2,1,0:T(8,128)(2,1)} %model_ref.1, bf16[2048,256]{1,0:T(8,128)(2,1)} %bitcast.6, f32[4,128,256]{2,1,0:T(8,128)} %obs_ref.1, f32[1,128]{1,0:T(1,128)} %bitcast.8), custom_call_target="tpu_custom_call" | custom-call | tf_op jit(solution)/shard_map/misfit_adjoint/pallas_call | solution.py:307
  44.3 1.2 %slice.3 = f32[1,1]{1,0:T(1,128)} slice(f32[8,128]{1,0:T(8,128)} %get-tuple-element.5), slice={[0:1], [0:1]} | slice | bytes 8 | tf_op jit(solution)/shard_map/slice | solution.py:347
  45.4 0.8 %copy.8 = f32[32,128]{0,1:T(8,128)S(1)} copy(f32[32,128]{1,0:T(8,128)} %get-tuple-element.4) | data formatting | bytes 32768 | tf_op jit(solution)/shard_map/misfit_adjoint/pallas_call | solution.py:307
  46.3 0.7 %reshape.19 = f32[1,16,256]{2,1,0:T(8,128)} reshape(f32[16,8,32]{2,1,0:T(8,128)S(1)} %copy.9) | data formatting | bytes 32768 | tf_op jit(solution)/shard_map/reshape | solution.py:346
  (1 shorter events, 0.0 us)

commit v2 on v1

v2 whole, which is shorter than its diff:
```python
import functools

import jax
import jax.numpy as jnp
from jax import lax
from jax.experimental import pallas as pl
from jax.experimental.pallas import tpu as pltpu
from jax.sharding import PartitionSpec as P

MESH = pl.DeviceIdType.MESH
F32 = jnp.float32
BF16 = jnp.bfloat16
NX = 4
NY = 4
B = 16
ORDER = (2, 1, 3)
PLANE = tuple((dx, dy) for dx in (2, 1, 3, 0) for dy in (2, 1, 3, 0) if dx or dy)


def nt(a, b):
    return lax.dot_general(a, b, (((1,), (1,)), ((), ())), preferred_element_type=F32)


def nn(a, b):
    return jnp.dot(a, b, preferred_element_type=F32)


def kernel(
    nz,
    scale,
    model_ref,
    kern_ref,
    obs_ref,
    weights_ref,
    out_ref,
    kv,
    kp,
    kt,
    w2,
    eye,
    swap,
    w_ref,
    mg,
    xp,
    ob,
    ot,
    sp,
    rs,
    zb,
    rf,
    rp,
    mq,
    mr,
    gs,
    gr,
    lsem,
    ssem,
    rsem,
):
    g = lax.axis_index("sens")
    par = lax.axis_index("par")
    z = par // (NX * NY)
    x = (par // NY) % NX
    y = par % NY

    def at_sens(d):
        return {"sens": (g + d) % 4, "par": par}

    def at_plane(dx, dy):
        return {"sens": g, "par": (z * NX + (x + dx) % NX) * NY + (y + dy) % NY}

    def at_z(d):
        return {"sens": g, "par": (((z + d) % nz) * NX + x) * NY + y}

    counter = [0]
    pending = []

    def phase(copies=3):
        base = counter[0]
        counter[0] += copies
        return base

    def send(number, src, dst, to):
        c = pltpu.make_async_remote_copy(
            src_ref=src,
            dst_ref=dst,
            send_sem=ssem.at[number],
            recv_sem=rsem.at[number],
            device_id=to,
            device_id_type=MESH,
        )
        c.start()
        pending.append(c)
        return c

    own = pltpu.make_async_copy(model_ref.at[0], mg.at[g], lsem.at[4])
    own.start()
    loads = []
    for n in range(4):
        c = pltpu.make_async_copy(kern_ref.at[pl.ds(512 * n, 512)], kv.at[pl.ds(512 * n, 512)], lsem.at[n])
        c.start()
        loads.append(c)
    load = pltpu.make_async_copy(
        obs_ref.at[x, :, pl.ds(pl.multiple_of(128 * (y // 2), 128), 128)], ob, lsem.at[5]
    )
    load.start()
    wload = pltpu.make_async_copy(weights_ref, w_ref, lsem.at[6])
    wload.start()

    barrier = pltpu.get_barrier_semaphore()
    zs = tuple(range(1, nz))
    for d in zs:
        pl.semaphore_signal(barrier, inc=1, device_id=at_z(d), device_id_type=MESH)
    for dx, dy in PLANE:
        pl.semaphore_signal(barrier, inc=1, device_id=at_plane(dx, dy), device_id_type=MESH)
    for d in ORDER:
        pl.semaphore_signal(barrier, inc=1, device_id=at_sens(d), device_id_type=MESH)

    rows = lax.broadcasted_iota(jnp.int32, (256, 256), 0)
    cols = lax.broadcasted_iota(jnp.int32, (256, 256), 1)
    eye[...] = jnp.where(rows == cols, 1.0, 0.0).astype(BF16)
    swap[...] = jnp.where((rows % 16) * 16 + rows // 16 == cols, 1.0, 0.0).astype(BF16)

    own.wait()
    pl.semaphore_wait(barrier, len(PLANE) + 3 + len(zs))
    ph = phase()
    gather = [send(ph + d - 1, mg.at[g], mg.at[g], at_sens(d)) for d in ORDER]

    for n in range(4):
        loads[n].wait()
        for m in (2 * n, 2 * n + 1):
            out = nn(swap[...], kv[pl.ds(256 * m, 256), :]).astype(BF16)
            kp[:, pl.ds(16 * m, 16), :] = out.reshape(16, 16, 256)

    for q in range(8):
        out = nt(eye[...], kp[2 * q : 2 * q + 2].reshape(256, 256)).astype(BF16)
        kt[2 * q] = out[:, :128]
        kt[2 * q + 1] = out[:, 128:]
    for c in range(8):
        lo = kt[:, 32 * c : 32 * c + 16, :].reshape(256, 128)
        hi = kt[:, 32 * c + 16 : 32 * c + 32, :].reshape(256, 128)
        out = nn(swap[...], jnp.concatenate([lo, hi], axis=1)).astype(BF16)
        w2[c] = out

    load.wait()
    wload.wait()
    ot[...] = ob[...].T

    for c in gather:
        c.wait_recv()

    lane = lax.broadcasted_iota(jnp.int32, (16, 256), 1)
    for v in range(4):
        m = mg[v].astype(F32)
        pieces = [m.astype(BF16)]
        for i in range(1, B):
            pieces.append(jnp.where(lane >= i, pltpu.roll(m, i, axis=1), 0.0).astype(BF16))
        stack = jnp.concatenate(pieces, axis=0)
        xp[v] = nt(eye[...], stack).astype(BF16)

    def predict(v):
        blocks = [None] * 16
        for c in range(8):
            out = nn(xp[v, 0 : B * (16 - 2 * c), :], w2[c])
            for b in range(16 - 2 * c):
                for e in (0, 1):
                    t = b + 2 * c + e
                    if t < 16:
                        part = out[B * b : B * b + B, 128 * e : 128 * e + 128]
                        blocks[t] = part if blocks[t] is None else blocks[t] + part
        return jnp.concatenate(blocks, axis=0)

    def quarter(n):
        return pl.ds(pl.multiple_of(64 * n, 64), 64)

    pha = phase(len(PLANE))
    ina = {}
    for dx in (2, 1, 3, 0):
        sp[dx] = predict((x + dx) % NX)
        for n, (px, dy) in enumerate(PLANE):
            if px == dx:
                ina[px, dy] = send(pha + n, sp.at[dx, quarter((y + dy) % NY)], rs.at[n], at_plane(dx, dy))
    block = sp[0, quarter(y), :]
    for first in (0, 4, 8, 12):
        group = range(first, min(first + 4, len(PLANE)))
        for n in group:
            ina[PLANE[n]].wait_recv()
        part = rs[first]
        for n in group[1:]:
            part = part + rs[n]
        block = block + part

    phz = phase()
    zb[z] = block
    inz = [send(phz + d - 1, zb.at[z], zb.at[z], at_z(d)) for d in zs]
    for c in inz:
        c.wait_recv()
    total = zb[0]
    for n in range(1, nz):
        total = total + zb[n]

    mismatch = total - ot[pl.ds(pl.multiple_of(64 * (y % 2), 64), 64), :]
    weighted = w_ref[...] * mismatch
    rf[x, quarter(y), :] = weighted.astype(BF16)
    phb = phase(len(PLANE))
    inb = {}
    for n, (dx, dy) in enumerate(PLANE):
        inb[dx, dy] = send(phb + n, rf.at[x, quarter(y)], rf.at[x, quarter(y)], at_plane(dx, dy))

    phy = phase()
    phx = phase()
    sq = (weighted * mismatch).reshape(8, 8, 128)
    sq = ((sq[0] + sq[1]) + (sq[2] + sq[3])) + ((sq[4] + sq[5]) + (sq[6] + sq[7]))
    mq[0] = sq
    mr[y] = sq
    iny = [send(phy + d - 1, mq.at[0], mr.at[y], at_plane(0, d)) for d in ORDER]

    rp[256:272, :] = jnp.zeros((16, 128), F32)
    group = lax.broadcasted_iota(jnp.int32, (B, 128), 1) // B

    def adjoint(v):
        rp[0:256, :] = rf[v].astype(F32)
        lhs = jnp.concatenate([rp[i : i + 256, :].astype(BF16) for i in range(B)], axis=1)
        rhs = jnp.concatenate(
            [
                jnp.concatenate([w2[:, B * i : B * i + B, 0:128], w2[:, B * i : B * i + B, 128:256]], axis=0).reshape(
                    256, 128
                )
                for i in range(B)
            ],
            axis=1,
        )
        out = nt(lhs, rhs)
        t = [out[B * b : B * b + B, :128] for b in range(16)]
        for b in range(15):
            t[b] = t[b] + out[B * b + B : B * b + 2 * B, 128:]
        for half in (0, 1):
            packed = None
            for r in range(-7, 8):
                picked = jnp.zeros((B, 128), F32)
                for c in range(max(0, -r), 8):
                    if 0 <= 2 * c + r < 8:
                        picked = jnp.where(group == c, t[2 * (2 * c + r) + half], picked)
                if r:
                    picked = pltpu.roll(picked, (B * r) % 128, axis=1)
                packed = picked if packed is None else packed + picked
            gs[v, B * half : B * half + B, :] = packed

    for dx in (0, 1, 3, 2):
        for dy in (0, 1, 3, 2):
            if (dx, dy) in inb:
                inb[dx, dy].wait_recv()
        adjoint((x + 4 - dx) % 4)
        if dx == 0:
            for c in iny:
                c.wait_recv()
            sq = (mr[0] + mr[1]) + (mr[2] + mr[3])
            mq[1] = sq
            mr[4 + x] = sq
            inx = [send(phx + d - 1, mq.at[1], mr.at[4 + x], at_plane(d, 0)) for d in ORDER]
    for c in inx:
        c.wait_recv()
    sq = (mr[4] + mr[5]) + (mr[6] + mr[7])

    phg = phase()
    ing = {}
    for d in ORDER:
        v = (g + d) % 4
        gs[v, 32:40, :] = sq
        ing[d] = send(phg + d - 1, gs.at[v], gr.at[d - 1], at_sens(d))
    for d in ORDER:
        ing[d].wait_recv()
    out_ref[0:32, :] = (gs[g, 0:32, :] + gr[0, 0:32]) + (gr[1, 0:32] + gr[2, 0:32])
    total = jnp.zeros((8, 128), F32)
    parts = [sq] + [gr[d - 1, 32:40] for d in (1, 2, 3)]
    for owner in range(4):
        for d in range(4):
            total = total + jnp.where((g + 4 - d) % 4 == owner, parts[d], 0.0)
    out_ref[32:40, :] = total * scale
    for c in pending:
        c.wait_send()


def finish(in_ref, grad_ref, mis_ref):
    series = in_ref[0:32, :].T
    for c in range(8):
        grad_ref[0, :, 32 * c : 32 * c + 32] = series[B * c : B * c + B, :]
    mis_ref[0, 0] = jnp.sum(in_ref[32:40, :])


def local(nz, scale, model, kern, observed, weights):
    sems = 45
    out = pl.pallas_call(
        functools.partial(kernel, nz, scale),
        out_shape=jax.ShapeDtypeStruct((40, 128), F32),
        in_specs=[pl.BlockSpec(memory_space=pltpu.HBM)] * 4,
        out_specs=pl.BlockSpec(memory_space=pltpu.VMEM),
        scratch_shapes=[
            pltpu.VMEM((2048, 256), BF16),
            pltpu.VMEM((16, 128, 256), BF16),
            pltpu.VMEM((16, 256, 128), BF16),
            pltpu.VMEM((8, 256, 256), BF16),
            pltpu.VMEM((256, 256), BF16),
            pltpu.VMEM((256, 256), BF16),
            pltpu.VMEM((1, 128), F32),
            pltpu.VMEM((4, 16, 256), BF16),
            pltpu.VMEM((4, 256, 256), BF16),
            pltpu.VMEM((128, 128), F32),
            pltpu.VMEM((128, 128), F32),
            pltpu.VMEM((4, 256, 128), F32),
            pltpu.VMEM((15, 64, 128), F32),
            pltpu.VMEM((nz, 64, 128), F32),
            pltpu.VMEM((4, 256, 128), BF16),
            pltpu.VMEM((272, 128), F32),
            pltpu.VMEM((2, 8, 128), F32),
            pltpu.VMEM((8, 8, 128), F32),
            pltpu.VMEM((4, 40, 128), F32),
            pltpu.VMEM((3, 40, 128), F32),
            pltpu.SemaphoreType.DMA((7,)),
            pltpu.SemaphoreType.DMA((sems,)),
            pltpu.SemaphoreType.DMA((sems,)),
        ],
        compiler_params=pltpu.CompilerParams(
            collective_id=0, has_side_effects=True, vmem_limit_bytes=24 * 1024 * 1024
        ),
        name="misfit_adjoint",
    )(*[pltpu.with_memory_space_constraint(a, pltpu.HBM) for a in (model, kern.reshape(2048, 256), observed, weights.reshape(1, 128))])
    gradient, misfit = pl.pallas_call(
        finish,
        out_shape=(jax.ShapeDtypeStruct((1, 16, 256), F32), jax.ShapeDtypeStruct((1, 1), F32)),
        in_specs=[pl.BlockSpec(memory_space=pltpu.VMEM)],
        out_specs=(pl.BlockSpec(memory_space=pltpu.VMEM), pl.BlockSpec(memory_space=pltpu.SMEM)),
        compiler_params=pltpu.CompilerParams(vmem_limit_bytes=4 * 1024 * 1024),
        name="finish",
    )(out)
    return gradient, misfit.reshape(())


def solution(mesh):
    nz = mesh.shape["par"] // (NX * NY)
    entries = 4 * 128 * mesh.shape["sens"] * 256
    return jax.shard_map(
        functools.partial(local, nz, 0.5 / entries),
        mesh=mesh,
        in_specs=(P("sens", "par", None), P("sens", "par", None), P(None, "sens", None), P("sens")),
        out_specs=(P("sens", "par", None), P()),
        check_vma=False,
    )
```

time: 47.2 us -> 42.4 us (0.90)
  local copies, waits for them, and re-layouts: 2.71 us -> 0 us
  Pallas kernels: 43.6 us -> 41.7 us
    pallas_call x1 -> x2, Pallas kernels: 43.6 us -> 41.7 us  [the longest x1 40.8 us: local(): pl.pallas_call(functools.partial(kernel, nz, scale), out_shape=jax.ShapeD...]
    slice x1 -> x0, local copies, waits for them, and re-layouts: 1.18 us -> none  [local(): return (gradient, mis[0, 0])]
    pallas_call x1 -> x0, local copies, waits for them, and re-layouts: 0.81 us -> none  [local(): pl.pallas_call(functools.partial(kernel, nz, scale), out_shape=(jax.Shape...]
    reshape x1 -> x0, local copies, waits for them, and re-layouts: 0.69 us -> none  [local(): gradient = grad.reshape(32, 8, 16).transpose(2, 1, 0).reshape(1, 16, 256)]
where the time goes in v2:
time: 42.4 us; the launch traced here: 42.3 us
  Pallas kernels  41.7 us (98%)
  between operations  0.64 us (2%)
    pallas_call x1, Pallas kernels, local(): pl.pallas_call(functools.partial(kernel, nz, scale), out_shape=jax.ShapeD...  40.8 us

profile of v2, /device:TPU:1, one launch (start us, length us, event | category | flops | bytes accessed | tf_op | source)
XLA Modules:
  0.0 42.3 jit_solution(9389913462307015542)
XLA Ops:
  0.6 40.8 %misfit_adjoint.1.in_ref = f32[40,128]{1,0:T(8,128)S(1)} custom-call(bf16[1,16,256]{2,1,0:T(8,128)(2,1)} %model_ref.1, bf16[2048,256]{1,0:T(8,128)(2,1)} %bitcast.3, f32[4,128,256]{2,1,0:T(8,128)} %obs_ref.1, f32[1,128]{1,0:T(1,128)} %bitcast.4), custom_call_target="tpu_custom_call" | custom-call | tf_op jit(solution)/shard_map/misfit_adjoint/pallas_call | solution.py:293
  41.5 0.8 %finish.1 = (f32[1,16,256]{2,1,0:T(8,128)}, f32[1,1]{1,0:T(1,128)}) custom-call(f32[40,128]{1,0:T(8,128)S(1)} %misfit_adjoint.1.in_ref), custom_call_target="tpu_custom_call" | custom-call | tf_op jit(solution)/shard_map/finish/pallas_call | solution.py:328

commit v3 on v2

--- a/solution.py
+++ b/solution.py
@@ -49,7 +49,6 @@
     zb,
     rf,
     rp,
-    mq,
     mr,
     gs,
     gr,
@@ -175,11 +174,12 @@
 
     pha = phase(len(PLANE))
     ina = {}
-    for dx in (2, 1, 3, 0):
-        sp[dx] = predict((x + dx) % NX)
+    for some in ((2, 1), (3, 0)):
+        for dx in some:
+            sp[dx] = predict((x + dx) % NX)
         for n, (px, dy) in enumerate(PLANE):
-            if px == dx:
-                ina[px, dy] = send(pha + n, sp.at[dx, quarter((y + dy) % NY)], rs.at[n], at_plane(dx, dy))
+            if px in some:
+                ina[px, dy] = send(pha + n, sp.at[px, quarter((y + dy) % NY)], rs.at[n], at_plane(px, dy))
     block = sp[0, quarter(y), :]
     for first in (0, 4, 8, 12):
         group = range(first, min(first + 4, len(PLANE)))
@@ -207,13 +207,11 @@
     for n, (dx, dy) in enumerate(PLANE):
         inb[dx, dy] = send(phb + n, rf.at[x, quarter(y)], rf.at[x, quarter(y)], at_plane(dx, dy))
 
-    phy = phase()
-    phx = phase()
-    sq = (weighted * mismatch).reshape(8, 8, 128)
-    sq = ((sq[0] + sq[1]) + (sq[2] + sq[3])) + ((sq[4] + sq[5]) + (sq[6] + sq[7]))
-    mq[0] = sq
-    mr[y] = sq
-    iny = [send(phy + d - 1, mq.at[0], mr.at[y], at_plane(0, d)) for d in ORDER]
+    sq = jnp.sum((weighted * mismatch).reshape(8, 8, 128), axis=0)
+    here = NY * x + y
+    mr[here] = jnp.sum(sq, axis=0, keepdims=True)
+    phm = phase(len(PLANE))
+    inm = [send(phm + n, mr.at[here], mr.at[here], at_plane(dx, dy)) for n, (dx, dy) in enumerate(PLANE)]
 
     rp[256:272, :] = jnp.zeros((16, 128), F32)
     group = lax.broadcasted_iota(jnp.int32, (B, 128), 1) // B
@@ -246,21 +244,16 @@
                 packed = picked if packed is None else packed + picked
             gs[v, B * half : B * half + B, :] = packed
 
-    for dx in (0, 1, 3, 2):
-        for dy in (0, 1, 3, 2):
-            if (dx, dy) in inb:
-                inb[dx, dy].wait_recv()
-        adjoint((x + 4 - dx) % 4)
-        if dx == 0:
-            for c in iny:
-                c.wait_recv()
-            sq = (mr[0] + mr[1]) + (mr[2] + mr[3])
-            mq[1] = sq
-            mr[4 + x] = sq
-            inx = [send(phx + d - 1, mq.at[1], mr.at[4 + x], at_plane(d, 0)) for d in ORDER]
-    for c in inx:
+    for c in inb.values():
         c.wait_recv()
-    sq = (mr[4] + mr[5]) + (mr[6] + mr[7])
+    for v in range(4):
+        adjoint(v)
+    for c in inm:
+        c.wait_recv()
+    parts = [mr[n] for n in range(NX * NY)]
+    while len(parts) > 1:
+        parts = [parts[n] + parts[n + 1] for n in range(0, len(parts), 2)]
+    sq = jnp.where(lax.broadcasted_iota(jnp.int32, (8, 128), 0) == 0, parts[0], 0.0)
 
     phg = phase()
     ing = {}
@@ -289,7 +282,7 @@
 
 
 def local(nz, scale, model, kern, observed, weights):
-    sems = 45
+    sems = 54
     out = pl.pallas_call(
         functools.partial(kernel, nz, scale),
         out_shape=jax.ShapeDtypeStruct((40, 128), F32),
@@ -312,8 +305,7 @@
             pltpu.VMEM((nz, 64, 128), F32),
             pltpu.VMEM((4, 256, 128), BF16),
             pltpu.VMEM((272, 128), F32),
-            pltpu.VMEM((2, 8, 128), F32),
-            pltpu.VMEM((8, 8, 128), F32),
+            pltpu.VMEM((16, 1, 128), F32),
             pltpu.VMEM((4, 40, 128), F32),
             pltpu.VMEM((3, 40, 128), F32),
             pltpu.SemaphoreType.DMA((7,)),

time: 42.4 us -> 41.1 us (0.969)
  Pallas kernels: 41.7 us -> 40.3 us
    pallas_call x1, Pallas kernels: 40.8 us -> 39.5 us  [local(): pl.pallas_call(functools.partial(kernel, nz, scale), out_shape=jax.ShapeD...]
where the time goes in v3:
time: 41.1 us; the launch traced here: 40.9 us
  Pallas kernels  40.3 us (98%)
  between operations  0.64 us (2%)
    pallas_call x1, Pallas kernels, local(): pl.pallas_call(functools.partial(kernel, nz, scale), out_shape=jax.ShapeD...  39.5 us

profile of v3, /device:TPU:1, one launch (start us, length us, event | category | flops | bytes accessed | tf_op | source)
XLA Modules:
  0.0 40.9 jit_solution(5637571943197328349)
XLA Ops:
  0.6 39.5 %misfit_adjoint.1.in_ref = f32[40,128]{1,0:T(8,128)S(1)} custom-call(bf16[1,16,256]{2,1,0:T(8,128)(2,1)} %model_ref.1, bf16[2048,256]{1,0:T(8,128)(2,1)} %bitcast.3, f32[4,128,256]{2,1,0:T(8,128)} %obs_ref.1, f32[1,128]{1,0:T(1,128)} %bitcast.4), custom_call_target="tpu_custom_call" | custom-call | tf_op jit(solution)/shard_map/misfit_adjoint/pallas_call | solution.py:286
  40.1 0.8 %finish.1 = (f32[1,16,256]{2,1,0:T(8,128)}, f32[1,1]{1,0:T(1,128)}) custom-call(f32[40,128]{1,0:T(8,128)S(1)} %misfit_adjoint.1.in_ref), custom_call_target="tpu_custom_call" | custom-call | tf_op jit(solution)/shard_map/finish/pallas_call | solution.py:320

commit v4 on v3

--- a/solution.py
+++ b/solution.py
@@ -120,16 +120,21 @@
     eye[...] = jnp.where(rows == cols, 1.0, 0.0).astype(BF16)
     swap[...] = jnp.where((rows % 16) * 16 + rows // 16 == cols, 1.0, 0.0).astype(BF16)
 
+    def spread(n):
+        loads[n].wait()
+        for m in (2 * n, 2 * n + 1):
+            out = nn(swap[...], kv[pl.ds(256 * m, 256), :]).astype(BF16)
+            kp[:, pl.ds(16 * m, 16), :] = out.reshape(16, 16, 256)
+
+    for n in range(2):
+        spread(n)
     own.wait()
     pl.semaphore_wait(barrier, len(PLANE) + 3 + len(zs))
     ph = phase()
     gather = [send(ph + d - 1, mg.at[g], mg.at[g], at_sens(d)) for d in ORDER]
 
-    for n in range(4):
-        loads[n].wait()
-        for m in (2 * n, 2 * n + 1):
-            out = nn(swap[...], kv[pl.ds(256 * m, 256), :]).astype(BF16)
-            kp[:, pl.ds(16 * m, 16), :] = out.reshape(16, 16, 256)
+    for n in range(2, 4):
+        spread(n)
 
     for q in range(8):
         out = nt(eye[...], kp[2 * q : 2 * q + 2].reshape(256, 256)).astype(BF16)
@@ -141,21 +146,20 @@
         out = nn(swap[...], jnp.concatenate([lo, hi], axis=1)).astype(BF16)
         w2[c] = out
 
-    load.wait()
-    wload.wait()
-    ot[...] = ob[...].T
-
-    for c in gather:
-        c.wait_recv()
-
     lane = lax.broadcasted_iota(jnp.int32, (16, 256), 1)
-    for v in range(4):
+
+    def shifts(v):
         m = mg[v].astype(F32)
         pieces = [m.astype(BF16)]
         for i in range(1, B):
             pieces.append(jnp.where(lane >= i, pltpu.roll(m, i, axis=1), 0.0).astype(BF16))
-        stack = jnp.concatenate(pieces, axis=0)
-        xp[v] = nt(eye[...], stack).astype(BF16)
+        xp[v] = nt(eye[...], jnp.concatenate(pieces, axis=0)).astype(BF16)
+
+    shifts(g)
+    for c in gather:
+        c.wait_recv()
+    for d in ORDER:
+        shifts((g + d) % 4)
 
     def predict(v):
         blocks = [None] * 16
@@ -180,6 +184,10 @@
         for n, (px, dy) in enumerate(PLANE):
             if px in some:
                 ina[px, dy] = send(pha + n, sp.at[px, quarter((y + dy) % NY)], rs.at[n], at_plane(px, dy))
+    load.wait()
+    wload.wait()
+    ot[...] = ob[...].T
+
     block = sp[0, quarter(y), :]
     for first in (0, 4, 8, 12):
         group = range(first, min(first + 4, len(PLANE)))
@@ -246,8 +254,8 @@
 
     for c in inb.values():
         c.wait_recv()
-    for v in range(4):
-        adjoint(v)
+    for d in ORDER:
+        adjoint((g + d) % 4)
     for c in inm:
         c.wait_recv()
     parts = [mr[n] for n in range(NX * NY)]
@@ -261,6 +269,7 @@
         v = (g + d) % 4
         gs[v, 32:40, :] = sq
         ing[d] = send(phg + d - 1, gs.at[v], gr.at[d - 1], at_sens(d))
+    adjoint(g)
     for d in ORDER:
         ing[d].wait_recv()
     out_ref[0:32, :] = (gs[g, 0:32, :] + gr[0, 0:32]) + (gr[1, 0:32] + gr[2, 0:32])

time: 41.1 us -> 40.9 us (level)
  no operation moved by 1% of the time
where the time goes in v4:
time: 40.9 us; the launch traced here: 40.8 us
  Pallas kernels  40.2 us (98%)
  between operations  0.64 us (2%)
    pallas_call x1, Pallas kernels, local(): pl.pallas_call(functools.partial(kernel, nz, scale), out_shape=jax.ShapeD...  39.4 us

profile of v4, /device:TPU:1, one launch (start us, length us, event | category | flops | bytes accessed | tf_op | source)
XLA Modules:
  0.0 40.8 jit_solution(17284885155456014058)
XLA Ops:
  0.6 39.4 %misfit_adjoint.1.in_ref = f32[40,128]{1,0:T(8,128)S(1)} custom-call(bf16[1,16,256]{2,1,0:T(8,128)(2,1)} %model_ref.1, bf16[2048,256]{1,0:T(8,128)(2,1)} %bitcast.3, f32[4,128,256]{2,1,0:T(8,128)} %obs_ref.1, f32[1,128]{1,0:T(1,128)} %bitcast.4), custom_call_target="tpu_custom_call" | custom-call | tf_op jit(solution)/shard_map/misfit_adjoint/pallas_call | solution.py:295
  40.0 0.8 %finish.1 = (f32[1,16,256]{2,1,0:T(8,128)}, f32[1,1]{1,0:T(1,128)}) custom-call(f32[40,128]{1,0:T(8,128)S(1)} %misfit_adjoint.1.in_ref), custom_call_target="tpu_custom_call" | custom-call | tf_op jit(solution)/shard_map/finish/pallas_call | solution.py:329

commit v5 on v4

--- a/solution.py
+++ b/solution.py
@@ -173,49 +173,63 @@
                         blocks[t] = part if blocks[t] is None else blocks[t] + part
         return jnp.concatenate(blocks, axis=0)
 
-    def quarter(n):
-        return pl.ds(pl.multiple_of(64 * n, 64), 64)
-
-    pha = phase(len(PLANE))
+    def half(n, h):
+        return pl.ds(pl.multiple_of(64 * n + 32 * h, 32), 32)
+
+    copies = len(PLANE)
+    pha = phase(2 * copies)
     ina = {}
+
+    def scatter(h, some):
+        for n, (dx, dy) in enumerate(PLANE):
+            if dx in some:
+                ina[h, n] = send(
+                    pha + copies * h + n,
+                    sp.at[dx, half((y + dy) % NY, h)],
+                    rs.at[copies * h + n],
+                    at_plane(dx, dy),
+                )
+
     for some in ((2, 1), (3, 0)):
         for dx in some:
             sp[dx] = predict((x + dx) % NX)
-        for n, (px, dy) in enumerate(PLANE):
-            if px in some:
-                ina[px, dy] = send(pha + n, sp.at[px, quarter((y + dy) % NY)], rs.at[n], at_plane(px, dy))
+        scatter(0, some)
+    scatter(1, (2, 1))
+    scatter(1, (3, 0))
+
     load.wait()
     wload.wait()
     ot[...] = ob[...].T
 
-    block = sp[0, quarter(y), :]
-    for first in (0, 4, 8, 12):
-        group = range(first, min(first + 4, len(PLANE)))
-        for n in group:
-            ina[PLANE[n]].wait_recv()
-        part = rs[first]
-        for n in group[1:]:
-            part = part + rs[n]
-        block = block + part
-
-    phz = phase()
-    zb[z] = block
-    inz = [send(phz + d - 1, zb.at[z], zb.at[z], at_z(d)) for d in zs]
-    for c in inz:
-        c.wait_recv()
-    total = zb[0]
-    for n in range(1, nz):
-        total = total + zb[n]
-
-    mismatch = total - ot[pl.ds(pl.multiple_of(64 * (y % 2), 64), 64), :]
-    weighted = w_ref[...] * mismatch
-    rf[x, quarter(y), :] = weighted.astype(BF16)
-    phb = phase(len(PLANE))
-    inb = {}
-    for n, (dx, dy) in enumerate(PLANE):
-        inb[dx, dy] = send(phb + n, rf.at[x, quarter(y)], rf.at[x, quarter(y)], at_plane(dx, dy))
-
-    sq = jnp.sum((weighted * mismatch).reshape(8, 8, 128), axis=0)
+    phz = phase(6)
+    inz = []
+    for h in (0, 1):
+        for n in range(copies):
+            ina[h, n].wait_recv()
+        parts = [sp[0, half(y, h), :]] + [rs[copies * h + n] for n in range(copies)]
+        while len(parts) > 1:
+            parts = [parts[n] + parts[n + 1] for n in range(0, len(parts), 2)]
+        zb[h, z] = parts[0]
+        inz.append([send(phz + 3 * h + d - 1, zb.at[h, z], zb.at[h, z], at_z(d)) for d in zs])
+
+    phb = phase(2 * copies)
+    inb = []
+    squares = []
+    for h in (0, 1):
+        for c in inz[h]:
+            c.wait_recv()
+        total = zb[h, 0]
+        for n in range(1, nz):
+            total = total + zb[h, n]
+        mismatch = total - ot[half(y % 2, h), :]
+        weighted = w_ref[...] * mismatch
+        rf[x, half(y, h), :] = weighted.astype(BF16)
+        for n, (dx, dy) in enumerate(PLANE):
+            mine = rf.at[x, half(y, h)]
+            inb.append(send(phb + copies * h + n, mine, mine, at_plane(dx, dy)))
+        squares.append(jnp.sum((weighted * mismatch).reshape(4, 8, 128), axis=0))
+
+    sq = squares[0] + squares[1]
     here = NY * x + y
     mr[here] = jnp.sum(sq, axis=0, keepdims=True)
     phm = phase(len(PLANE))
@@ -252,7 +266,7 @@
                 packed = picked if packed is None else packed + picked
             gs[v, B * half : B * half + B, :] = packed
 
-    for c in inb.values():
+    for c in inb:
         c.wait_recv()
     for d in ORDER:
         adjoint((g + d) % 4)
@@ -291,7 +305,7 @@
 
 
 def local(nz, scale, model, kern, observed, weights):
-    sems = 54
+    sems = 87
     out = pl.pallas_call(
         functools.partial(kernel, nz, scale),
         out_shape=jax.ShapeDtypeStruct((40, 128), F32),
@@ -310,8 +324,8 @@
             pltpu.VMEM((128, 128), F32),
             pltpu.VMEM((128, 128), F32),
             pltpu.VMEM((4, 256, 128), F32),
-            pltpu.VMEM((15, 64, 128), F32),
-            pltpu.VMEM((nz, 64, 128), F32),
+            pltpu.VMEM((30, 32, 128), F32),
+            pltpu.VMEM((2, nz, 32, 128), F32),
             pltpu.VMEM((4, 256, 128), BF16),
             pltpu.VMEM((272, 128), F32),
             pltpu.VMEM((16, 1, 128), F32),

time: 40.9 us -> 40.7 us (level)
  no operation moved by 1% of the time
where the time goes in v5:
time: 40.7 us; the launch traced here: 40.6 us
  Pallas kernels  40 us (98%)
  between operations  0.64 us (2%)
    pallas_call x1, Pallas kernels, local(): pl.pallas_call(functools.partial(kernel, nz, scale), out_shape=jax.ShapeD...  39.2 us

profile of v5, /device:TPU:1, one launch (start us, length us, event | category | flops | bytes accessed | tf_op | source)
XLA Modules:
  0.0 40.6 jit_solution(13178845966170851343)
XLA Ops:
  0.6 39.2 %misfit_adjoint.1.in_ref = f32[40,128]{1,0:T(8,128)S(1)} custom-call(bf16[1,16,256]{2,1,0:T(8,128)(2,1)} %model_ref.1, bf16[2048,256]{1,0:T(8,128)(2,1)} %bitcast.3, f32[4,128,256]{2,1,0:T(8,128)} %obs_ref.1, f32[1,128]{1,0:T(1,128)} %bitcast.4), custom_call_target="tpu_custom_call" | custom-call | tf_op jit(solution)/shard_map/misfit_adjoint/pallas_call | solution.py:309
  39.8 0.8 %finish.1 = (f32[1,16,256]{2,1,0:T(8,128)}, f32[1,1]{1,0:T(1,128)}) custom-call(f32[40,128]{1,0:T(8,128)S(1)} %misfit_adjoint.1.in_ref), custom_call_target="tpu_custom_call" | custom-call | tf_op jit(solution)/shard_map/finish/pallas_call | solution.py:343
